TPU v7x, 128 devices: a whole 4x4x4 slice. The times are simulated.
128 devices in a mesh: cam: 16 (over y, x), pts: 8 (over z, core).
Axes of the slice: x: 4, y: 4, z: 4, core: 2. Of those that a mesh axis runs over, the one named last changes fastest.
Arguments:
- rhs: float32 [9, 131072], P(None, 'cam'), may hold values from -6 to 6
- cam_block: float32 [9, 9, 131072], P(None, None, 'cam'), as said below
- coupling: bfloat16 [512, 144, 12288], P('pts', None, 'cam'), may hold values from -0.03125 to 0.03125
- point_inverse: float32 [3, 3, 32768], P(None, None, 'pts'), as said below
- precond: float32 [9, 9, 131072], P(None, None, 'cam'), as said below
- tile_index: int32 [512, 64], P('pts', 'cam'), may hold values from 0 to 511
- tile_count: int32 [512, 16], P('pts', 'cam'), may hold values from 1 to 4, as said below
Outputs:
- solution: float32 [9, 131072], P(None, 'cam')
- residual: float32 [9, 131072], P(None, 'cam')
Inputs may be any that keep to these rules, and one draw needn't show every extreme that they name: `tile_count`: every entry is at least 1 and at most 4; both ends occur. `cam_block`: symmetric with a dominant positive diagonal for each camera. `precond`: symmetric with a dominant positive diagonal for each camera. `point_inverse`: symmetric with a dominant positive diagonal for each point.
All inputs are finite; a program needn't handle non-finite values.
Results may differ from a plain program's by a relative error of at most 0.0024.
Values may be sent and summed in bfloat16 or wider, within the bound.
A program may use at most 128 MiB of HBM per device.

v0:
```python
import jax
import jax.numpy as jnp
from jax import lax
from jax.sharding import PartitionSpec as P

ITERS = 3


def camera_tiles(vector):
    comps, count = vector.shape
    return (
        vector.reshape(comps, count // 16, 16).transpose(1, 0, 2).reshape(count // 16, comps * 16)
    )


def camera_cols(tiles):
    count = tiles.shape[0]
    return tiles.reshape(count, 9, 16).transpose(1, 0, 2).reshape(9, count * 16)


def point_cols(tiles):
    count = tiles.shape[0]
    return tiles.reshape(count, 3, 64).transpose(1, 0, 2).reshape(3, count * 64)


def point_tiles(vector):
    count = vector.shape[1] // 64
    return vector.reshape(3, count, 64).transpose(1, 0, 2).reshape(count, 192)


def per_device(rhs, cam_block, coupling, point_inverse, precond, tile_index, tile_count):
    tiles_here, slot_count = tile_index.shape
    cam_count = rhs.shape[1] // 16
    blocks = coupling.reshape(tiles_here, 144, slot_count, 192)
    usable = (jnp.arange(slot_count)[None, :] < tile_count).astype(jnp.bfloat16)
    flat_index = tile_index.reshape(-1)
    onehot_t = (jnp.arange(cam_count)[:, None] == flat_index[None, :]).astype(
        jnp.float32
    ) * usable.reshape(1, -1).astype(jnp.float32)

    def global_sum(value):
        return lax.psum(value, "cam")

    solution = jnp.zeros_like(rhs)
    residual = rhs
    precond_res = jnp.sum(precond * residual[None, :, :], axis=1)
    direction = precond_res
    inner_now = global_sum(jnp.sum(residual * precond_res))
    for iteration in range(ITERS):
        dir_rows = jnp.take(
            camera_tiles(direction.astype(jnp.bfloat16)), flat_index, axis=0
        ).reshape(tiles_here, slot_count, 144)
        dir_rows = dir_rows * usable[:, :, None]
        point_part = jnp.einsum(
            "tckp,tkc->tp", blocks, dir_rows, preferred_element_type=jnp.float32
        )
        point_part = point_cols(point_part)
        summed = lax.psum(point_part.astype(jnp.bfloat16), "cam").astype(jnp.float32)
        solved = jnp.sum(point_inverse * summed[None, :, :], axis=1).astype(jnp.bfloat16)
        contrib = jnp.einsum(
            "tckp,tp->tkc", blocks, point_tiles(solved), preferred_element_type=jnp.float32
        )
        cam_part = jnp.dot(
            onehot_t,
            contrib.reshape(-1, 144),
            precision=lax.Precision.HIGHEST,
            preferred_element_type=jnp.float32,
        )
        image = jnp.sum(cam_block * direction[None, :, :], axis=1) - lax.psum(
            camera_cols(cam_part).astype(jnp.bfloat16), "pts"
        ).astype(jnp.float32)
        step_size = inner_now / global_sum(jnp.sum(direction * image))
        solution = solution + step_size * direction
        residual = residual - step_size * image
        if iteration + 1 < ITERS:
            precond_res = jnp.sum(precond * residual[None, :, :], axis=1)
            inner_new = global_sum(jnp.sum(residual * precond_res))
            direction = precond_res + inner_new / inner_now * direction
            inner_now = inner_new
    return (solution, residual)


def solution(mesh):
    in_specs = (
        P(None, "cam"),
        P(None, None, "cam"),
        P("pts", None, "cam"),
        P(None, None, "pts"),
        P(None, None, "cam"),
        P("pts", "cam"),
        P("pts", "cam"),
    )
    out_specs = (P(None, "cam"), P(None, "cam"))
    return jax.shard_map(
        per_device, mesh=mesh, in_specs=in_specs, out_specs=out_specs, check_vma=False
    )
```

profile of v0, /device:TPU:0, one launch (start us, length us, event | category | flops | bytes accessed | tf_op | source)
XLA Modules:
  0.0 773.3 jit_solution(13054918832175976593)
XLA Ops:
  7.2 0.8 copy.25
  8.1 3.4 multiply_reduce_fusion.5
  11.6 1.1 convert_element_type.149
  13.2 1.2 gather_fusion
  14.6 35.9 %reshape.168 = bf16[64,144,4,192]{3,2,1,0:T(4,128)(2,1)} reshape(bf16[64,144,768]{2,1,0:T(8,128)(2,1)} %param.11) | data formatting | bytes 28311552 | tf_op jit(solution)/shard_map/reshape | solution.py:34
  50.6 9.1 %fusion.7 = bf16[64,1,192,1]{2,1,3,0:T(2,128)(2,1)S(1)} fusion(bf16[64,144,4,192]{3,2,1,0:T(4,128)(2,1)} %reshape.168, bf16[64,4,144,1]{2,1,0,3:T(4,128)(2,1)S(1)} %multiply_bitcast_fusion.2), kind=kOutput, calls=%fused_computation.13 | convolution fusion | flops 14155776 | bytes 14254080 | tf_op jit(solution)/shard_map/tckp,tkc->tp/dot_general | solution.py:54
  60.1 75.1 %psum.85 = bf16[3,4096]{1,0:T(4,128)(2,1)S(1)} all-reduce(bf16[3,4096]{1,0:T(4,128)(2,1)S(1)} %convert_element_type.154), channel_id=1, replica_groups=mesh['cam'=16,'pts'=8] {'cam'}, use_global_device_ids=true, to_apply=%region_4.6 | all-reduce | flops 12288 | bytes 49152 | tf_op jit(solution)/shard_map/psum | solution.py:58
  135.7 16.4 %fusion = f32[64,144,4]{2,1,0:T(8,128)} fusion(f32[64,192]{1,0:T(8,128)S(1)} %copy.66, bf16[64,144,4,192]{3,2,1,0:T(4,128)(2,1)} %reshape.168), kind=kLoop, calls=%fused_computation.6 | loop fusion | flops 21196800 | bytes 14352384
  152.1 4.1 copy.51
  156.5 0.8 fusion.9
  157.8 2.5 convert_element_type.160
  160.4 3.3 multiply_reduce_fusion.4
  163.7 54.2 %all-reduce.5.cloned.1.call-done = bf16[9,8192]{1,0:T(8,128)(2,1)} async-done(((bf16[9,8192]{1,0:T(8,128)(2,1)}), bf16[9,8192]{1,0:T(8,128)(2,1)}) %all-reduce.5.cloned.1.call-update) | async-done | bytes 147472 | tf_op jit(solution)/shard_map/psum | solution.py:69
  217.9 1.7 multiply_reduce_fusion.10
  219.6 40.9 %all-reduce = (f32[]{:T(128)}, f32[]{:T(128)}) all-reduce(f32[]{:T(128)} %get-tuple-element.4, f32[]{:T(128)} %get-tuple-element.3), channel_id=1, replica_groups=mesh['cam'=16,'pts'=8] {'cam'}, use_global_device_ids=true, to_apply=%region_2.0 | all-reduce | flops 2 | bytes 16 | tf_op jit(solution)/shard_map/psum | solution.py:42
  261.8 1.0 multiply_subtract_fusion.2
  262.9 3.3 multiply_reduce_fusion.3
  266.9 36.6 %psum.88 = f32[]{:T(128)} all-reduce(f32[]{:T(128)} %multiply_reduce_fusion.9), channel_id=1, replica_groups=mesh['cam'=16,'pts'=8] {'cam'}, use_global_device_ids=true, to_apply=%region_11.13 | all-reduce | flops 1 | bytes 8 | tf_op jit(solution)/shard_map/psum | solution.py:42
  304.8 1.1 convert_element_type.163
  306.4 1.2 gather_fusion.1
  307.9 9.1 %fusion.5 = bf16[64,1,192,1]{2,1,3,0:T(2,128)(2,1)S(1)} fusion(bf16[64,144,4,192]{3,2,1,0:T(4,128)(2,1)} %reshape.168, bf16[64,4,144,1]{2,1,0,3:T(4,128)(2,1)S(1)} %multiply_bitcast_fusion.1), kind=kOutput, calls=%fused_computation.11 | convolution fusion | flops 14155776 | bytes 14254080 | tf_op jit(solution)/shard_map/tckp,tkc->tp/dot_general | solution.py:54
  317.3 71.4 %psum.89 = bf16[3,4096]{1,0:T(4,128)(2,1)S(1)} all-reduce(bf16[3,4096]{1,0:T(4,128)(2,1)S(1)} %convert_element_type.167), channel_id=1, replica_groups=mesh['cam'=16,'pts'=8] {'cam'}, use_global_device_ids=true, to_apply=%region_13.15 | all-reduce | flops 12288 | bytes 49152 | tf_op jit(solution)/shard_map/psum | solution.py:58
  389.2 16.4 %fusion.1 = f32[64,144,4]{2,1,0:T(8,128)} fusion(f32[64,192]{1,0:T(8,128)S(1)} %copy.67, bf16[64,144,4,192]{3,2,1,0:T(4,128)(2,1)} %reshape.168), kind=kLoop, calls=%fused_computation.7 | loop fusion | flops 21196800 | bytes 14352384
  405.6 4.1 copy.58
  409.9 0.8 fusion.10
  411.2 2.5 convert_element_type.173
  413.8 3.3 multiply_reduce_fusion.2
  417.1 50.6 %all-reduce.7.cloned.1.call-done = bf16[9,8192]{1,0:T(8,128)(2,1)} async-done(((bf16[9,8192]{1,0:T(8,128)(2,1)}), bf16[9,8192]{1,0:T(8,128)(2,1)}) %all-reduce.7.cloned.1.call-update) | async-done | bytes 147472 | tf_op jit(solution)/shard_map/psum | solution.py:69
  467.7 1.7 multiply_reduce_fusion.8
  469.4 41.1 %psum.91 = f32[]{:T(128)} all-reduce(f32[]{:T(128)} %multiply_reduce_fusion.8), channel_id=1, replica_groups=mesh['cam'=16,'pts'=8] {'cam'}, use_global_device_ids=true, to_apply=%region_17.19 | all-reduce | flops 1 | bytes 8 | tf_op jit(solution)/shard_map/psum | solution.py:42
  511.7 1.0 multiply_subtract_fusion.1
  512.8 3.3 multiply_reduce_fusion.1
  516.8 36.1 %psum.92 = f32[]{:T(128)} all-reduce(f32[]{:T(128)} %multiply_reduce_fusion.7), channel_id=1, replica_groups=mesh['cam'=16,'pts'=8] {'cam'}, use_global_device_ids=true, to_apply=%region_20.22 | all-reduce | flops 1 | bytes 8 | tf_op jit(solution)/shard_map/psum | solution.py:42
  554.1 0.8 fusion.35
  554.9 1.9 add.63
  556.9 1.0 copy.38
  557.9 1.0 copy.39
  558.9 1.2 gather_fusion.2
  560.4 9.1 %fusion.3 = bf16[64,1,192,1]{2,1,3,0:T(2,128)(2,1)S(1)} fusion(bf16[64,144,4,192]{3,2,1,0:T(4,128)(2,1)} %reshape.168, bf16[64,4,144,1]{2,1,0,3:T(4,128)(2,1)S(1)} %multiply_bitcast_fusion), kind=kOutput, calls=%fused_computation.9 | convolution fusion | flops 14155776 | bytes 14254080 | tf_op jit(solution)/shard_map/tckp,tkc->tp/dot_general | solution.py:54
  569.8 71.7 %psum.93 = bf16[3,4096]{1,0:T(4,128)(2,1)S(1)} all-reduce(bf16[3,4096]{1,0:T(4,128)(2,1)S(1)} %convert_element_type.178), channel_id=1, replica_groups=mesh['cam'=16,'pts'=8] {'cam'}, use_global_device_ids=true, to_apply=%region_22.24 | all-reduce | flops 12288 | bytes 49152 | tf_op jit(solution)/shard_map/psum | solution.py:58
  642.1 16.4 %fusion.2 = f32[64,144,4]{2,1,0:T(8,128)} fusion(f32[64,192]{1,0:T(8,128)S(1)} %copy.68, bf16[64,144,4,192]{3,2,1,0:T(4,128)(2,1)} %reshape.168), kind=kLoop, calls=%fused_computation.8 | loop fusion | flops 21196800 | bytes 14352384
  658.4 4.1 copy.65
  664.0 2.5 convert_element_type.184
  666.6 3.3 multiply_reduce_fusion
  669.9 50.6 %all-reduce.9.cloned.1.call-done = bf16[9,8192]{1,0:T(8,128)(2,1)} async-done(((bf16[9,8192]{1,0:T(8,128)(2,1)}), bf16[9,8192]{1,0:T(8,128)(2,1)}) %all-reduce.9.cloned.1.call-update) | async-done | bytes 147472 | tf_op jit(solution)/shard_map/psum | solution.py:69
  720.5 1.7 multiply_reduce_fusion.6
  722.2 40.9 %psum.95 = f32[]{:T(128)} all-reduce(f32[]{:T(128)} %multiply_reduce_fusion.6), channel_id=1, replica_groups=mesh['cam'=16,'pts'=8] {'cam'}, use_global_device_ids=true, to_apply=%region_26.28 | all-reduce | flops 1 | bytes 8 | tf_op jit(solution)/shard_map/psum | solution.py:42
  764.5 2.1 multiply_subtract_fusion
  (72 shorter events, 9.2 us)
Async XLA Ops:
  7.2 210.7 %all-reduce.5.cloned.1.call-start = ((), (), s32[]{:S(2)}) async-start(), calls=%async_computation | async-start | bytes 524288 | tf_op jit(solution)/shard_map/psum | solution.py:69
  8.1 6.4 copy-start.2
  50.6 84.6 %copy-start.1 = (f32[3,3,4096]{2,1,0:T(4,128)S(1)}, f32[3,3,4096]{2,1,0:T(4,128)}, u32[]{:S(2)}) copy-start(f32[3,3,4096]{2,1,0:T(4,128)} %param.12) | copy-start | bytes 442372
  156.4 61.4 %copy-start = (f32[9,8192]{1,0:T(8,128)S(1)}, f32[9,8192]{1,0:T(8,128)}, u32[]{:S(2)}) copy-start(f32[9,8192]{1,0:T(8,128)} %param.9) | copy-start | bytes 884740
  160.4 307.3 %all-reduce.7.cloned.1.call-start = ((), (), s32[]{:S(2)}) async-start(), calls=%async_computation.1 | async-start | bytes 524288 | tf_op jit(solution)/shard_map/psum | solution.py:69
  413.7 306.8 %all-reduce.9.cloned.1.call-start = ((), (), s32[]{:S(2)}) async-start(), calls=%async_computation.2 | async-start | bytes 524288 | tf_op jit(solution)/shard_map/psum | solution.py:69
Sparse Core Ops, SparseCore 0:
  160.5 57.3 all-reduce.4
  413.8 53.7 all-reduce.6
  666.7 53.7 all-reduce.8
where the time goes:
time: 781 us; the launch traced here: 773 us
  blocking collectives  414 us (53%)
  waiting for transfers between devices  155 us (20%)
  other arithmetic  82 us (10%)
  local copies, waits for them, and re-layouts  71.4 us (9%)
  matrix products  29.6 us (4%)
  between operations  20.8 us (3%)
    psum x3, blocking collectives, per_device(): lax.psum(point_part.astype(jnp.bfloat16), 'cam').astype(jnp.float32)  218 us
    psum x5, blocking collectives, global_sum(): return lax.psum(value, 'cam')  196 us
    psum x3, waiting for transfers between devices, per_device(): lax.psum(camera_cols(cam_part).astype(jnp.bfloat16), 'pts')  155 us
    unnamed x6, other arithmetic  49.2 us
    reshape x1, local copies, waits for them, and re-layouts, per_device(): blocks = coupling.reshape(tiles_here, 144, slot_count, 192)  35.9 us
    dot_general x3, matrix products, per_device(): jnp.einsum('tckp,tkc->tp', blocks, dir_rows, preferred_element_type=jnp.f...  27.4 us
  transfers between devices with their start and end apart: 3, of which 3 were waited for; matrix products, arithmetic and copies ran while one was open for 1% of the time, Pallas kernels for 0%

commit v1 on v0

--- a/solution.py
+++ b/solution.py
@@ -4,6 +4,11 @@
 from jax.sharding import PartitionSpec as P
 
 ITERS = 3
+
+
+def gather_and_add(x, axis):
+    parts = lax.all_gather(x, axis)
+    return jnp.sum(parts, axis=0)
 
 
 def camera_tiles(vector):
@@ -55,7 +60,7 @@
             "tckp,tkc->tp", blocks, dir_rows, preferred_element_type=jnp.float32
         )
         point_part = point_cols(point_part)
-        summed = lax.psum(point_part.astype(jnp.bfloat16), "cam").astype(jnp.float32)
+        summed = gather_and_add(point_part.astype(jnp.bfloat16), "cam").astype(jnp.float32)
         solved = jnp.sum(point_inverse * summed[None, :, :], axis=1).astype(jnp.bfloat16)
         contrib = jnp.einsum(
             "tckp,tp->tkc", blocks, point_tiles(solved), preferred_element_type=jnp.float32

time: 781 us -> 641 us (0.82)
  blocking collectives: 414 us -> 266 us
  waiting for transfers between devices: 155 us -> 163 us
    psum x3 -> x0, blocking collectives: 218 us -> none  [per_device(): lax.psum(point_part.astype(jnp.bfloat16), 'cam').astype(jnp.float32)]
    all_gather x0 -> x3, blocking collectives: none -> 70.6 us  [gather_and_add(): parts = lax.all_gather(x, axis)]
    psum x3, waiting for transfers between devices: 155 us -> 163 us  [per_device(): lax.psum(camera_cols(cam_part).astype(jnp.bfloat16), 'pts')]
  transfers between devices with their start and end apart: 3 -> 3, of which waited for: 3 -> 3; matrix products, arithmetic and copies ran while one was open for 1% -> 2% of each run, Pallas kernels for 0% -> 0%
where the time goes in v1:
time: 641 us; the launch traced here: 634 us
  blocking collectives  266 us (41%)
  waiting for transfers between devices  163 us (25%)
  other arithmetic  82.6 us (13%)
  local copies, waits for them, and re-layouts  71.4 us (11%)
  matrix products  29.6 us (5%)
  between operations  20.9 us (3%)
    psum x5, blocking collectives, global_sum(): return lax.psum(value, 'cam')  196 us
    psum x3, waiting for transfers between devices, per_device(): lax.psum(camera_cols(cam_part).astype(jnp.bfloat16), 'pts')  163 us
    all_gather x3, blocking collectives, gather_and_add(): parts = lax.all_gather(x, axis)  70.6 us
    unnamed x6, other arithmetic  49.2 us
    reshape x1, local copies, waits for them, and re-layouts, per_device(): blocks = coupling.reshape(tiles_here, 144, slot_count, 192)  35.9 us
    dot_general x3, matrix products, per_device(): jnp.einsum('tckp,tkc->tp', blocks, dir_rows, preferred_element_type=jnp.f...  27.4 us
  transfers between devices with their start and end apart: 3, of which 3 were waited for; matrix products, arithmetic and copies ran while one was open for 2% of the time, Pallas kernels for 0%

profile of v1, /device:TPU:0, one launch (start us, length us, event | category | flops | bytes accessed | tf_op | source)
XLA Modules:
  0.0 634.2 jit_solution(16441384432490718578)
XLA Ops:
  7.2 0.8 copy.47
  8.1 3.4 multiply_reduce_fusion.5
  11.6 1.1 convert_element_type.188
  13.2 1.2 gather_fusion
  14.6 35.9 %reshape.204 = bf16[64,144,4,192]{3,2,1,0:T(4,128)(2,1)} reshape(bf16[64,144,768]{2,1,0:T(8,128)(2,1)} %param.11) | data formatting | bytes 28311552 | tf_op jit(solution)/shard_map/reshape | solution.py:39
  50.6 9.1 %fusion.7 = bf16[64,1,192,1]{2,1,3,0:T(2,128)(2,1)S(1)} fusion(bf16[64,144,4,192]{3,2,1,0:T(4,128)(2,1)} %reshape.204, bf16[64,4,144,1]{2,1,0,3:T(4,128)(2,1)S(1)} %multiply_bitcast_fusion.2), kind=kOutput, calls=%fused_computation.13 | convolution fusion | flops 14155776 | bytes 14254080 | tf_op jit(solution)/shard_map/tckp,tkc->tp/dot_general | solution.py:59
  60.1 24.6 %all_gather.12 = bf16[16,3,4096]{2,1,0:T(4,128)(2,1)S(1)} all-gather(bf16[1,3,4096]{2,1,0:T(4,128)(2,1)S(1)} %convert_element_type.193), channel_id=1, replica_groups=mesh['cam'=16,'pts'=8] {'cam'}, dimensions={0}, use_global_device_ids=true | all-gather | bytes 417792 | tf_op jit(solution)/shard_map/all_gather | solution.py:10
  85.5 16.4 %fusion = f32[64,144,4]{2,1,0:T(8,128)} fusion(f32[64,192]{1,0:T(8,128)S(1)} %copy.88, bf16[64,144,4,192]{3,2,1,0:T(4,128)(2,1)} %reshape.204), kind=kLoop, calls=%fused_computation.6 | loop fusion | flops 21196800 | bytes 14352384
  101.9 4.1 copy.73
  106.3 0.8 fusion.9
  107.6 2.5 convert_element_type.199
  110.2 3.3 multiply_reduce_fusion.4
  113.5 57.1 %all-reduce.5.cloned.1.call-done = bf16[9,8192]{1,0:T(8,128)(2,1)} async-done(((bf16[9,8192]{1,0:T(8,128)(2,1)}), bf16[9,8192]{1,0:T(8,128)(2,1)}) %all-reduce.5.cloned.1.call-update) | async-done | bytes 147472 | tf_op jit(solution)/shard_map/psum | solution.py:74
  170.5 1.7 multiply_reduce_fusion.10
  172.2 40.9 %all-reduce = (f32[]{:T(128)}, f32[]{:T(128)}) all-reduce(f32[]{:T(128)} %get-tuple-element.4, f32[]{:T(128)} %get-tuple-element.3), channel_id=1, replica_groups=mesh['cam'=16,'pts'=8] {'cam'}, use_global_device_ids=true, to_apply=%region_2.0 | all-reduce | flops 2 | bytes 16 | tf_op jit(solution)/shard_map/psum | solution.py:47
  214.5 1.0 multiply_subtract_fusion.2
  215.5 3.3 multiply_reduce_fusion.3
  219.6 36.6 %psum.66 = f32[]{:T(128)} all-reduce(f32[]{:T(128)} %multiply_reduce_fusion.9), channel_id=1, replica_groups=mesh['cam'=16,'pts'=8] {'cam'}, use_global_device_ids=true, to_apply=%region_11.13 | all-reduce | flops 1 | bytes 8 | tf_op jit(solution)/shard_map/psum | solution.py:47
  257.5 1.1 convert_element_type.202
  259.1 1.2 gather_fusion.1
  260.5 9.1 %fusion.5 = bf16[64,1,192,1]{2,1,3,0:T(2,128)(2,1)S(1)} fusion(bf16[64,144,4,192]{3,2,1,0:T(4,128)(2,1)} %reshape.204, bf16[64,4,144,1]{2,1,0,3:T(4,128)(2,1)S(1)} %multiply_bitcast_fusion.1), kind=kOutput, calls=%fused_computation.11 | convolution fusion | flops 14155776 | bytes 14254080 | tf_op jit(solution)/shard_map/tckp,tkc->tp/dot_general | solution.py:59
  270.0 22.9 %all_gather.13 = bf16[16,3,4096]{2,1,0:T(4,128)(2,1)S(1)} all-gather(bf16[1,3,4096]{2,1,0:T(4,128)(2,1)S(1)} %convert_element_type.206), channel_id=1, replica_groups=mesh['cam'=16,'pts'=8] {'cam'}, dimensions={0}, use_global_device_ids=true | all-gather | bytes 417792 | tf_op jit(solution)/shard_map/all_gather | solution.py:10
  293.6 16.4 %fusion.1 = f32[64,144,4]{2,1,0:T(8,128)} fusion(f32[64,192]{1,0:T(8,128)S(1)} %copy.89, bf16[64,144,4,192]{3,2,1,0:T(4,128)(2,1)} %reshape.204), kind=kLoop, calls=%fused_computation.7 | loop fusion | flops 21196800 | bytes 14352384
  310.0 4.1 copy.80
  315.6 2.5 convert_element_type.212
  318.2 3.3 multiply_reduce_fusion.2
  321.5 53.1 %all-reduce.7.cloned.1.call-done = bf16[9,8192]{1,0:T(8,128)(2,1)} async-done(((bf16[9,8192]{1,0:T(8,128)(2,1)}), bf16[9,8192]{1,0:T(8,128)(2,1)}) %all-reduce.7.cloned.1.call-update) | async-done | bytes 147472 | tf_op jit(solution)/shard_map/psum | solution.py:74
  374.6 1.7 multiply_reduce_fusion.8
  376.2 41.1 %psum.68 = f32[]{:T(128)} all-reduce(f32[]{:T(128)} %multiply_reduce_fusion.8), channel_id=1, replica_groups=mesh['cam'=16,'pts'=8] {'cam'}, use_global_device_ids=true, to_apply=%region_17.19 | all-reduce | flops 1 | bytes 8 | tf_op jit(solution)/shard_map/psum | solution.py:47
  418.6 1.0 multiply_subtract_fusion.1
  419.6 3.3 multiply_reduce_fusion.1
  423.7 36.1 %psum.69 = f32[]{:T(128)} all-reduce(f32[]{:T(128)} %multiply_reduce_fusion.7), channel_id=1, replica_groups=mesh['cam'=16,'pts'=8] {'cam'}, use_global_device_ids=true, to_apply=%region_20.22 | all-reduce | flops 1 | bytes 8 | tf_op jit(solution)/shard_map/psum | solution.py:47
  461.0 0.8 fusion.35
  461.8 1.9 add.57
  463.7 1.0 copy.60
  464.8 1.0 copy.61
  465.8 1.2 gather_fusion.2
  467.3 9.1 %fusion.3 = bf16[64,1,192,1]{2,1,3,0:T(2,128)(2,1)S(1)} fusion(bf16[64,144,4,192]{3,2,1,0:T(4,128)(2,1)} %reshape.204, bf16[64,4,144,1]{2,1,0,3:T(4,128)(2,1)S(1)} %multiply_bitcast_fusion), kind=kOutput, calls=%fused_computation.9 | convolution fusion | flops 14155776 | bytes 14254080 | tf_op jit(solution)/shard_map/tckp,tkc->tp/dot_general | solution.py:59
  476.7 23.1 %all_gather.14 = bf16[16,3,4096]{2,1,0:T(4,128)(2,1)S(1)} all-gather(bf16[1,3,4096]{2,1,0:T(4,128)(2,1)S(1)} %convert_element_type.217), channel_id=1, replica_groups=mesh['cam'=16,'pts'=8] {'cam'}, dimensions={0}, use_global_device_ids=true | all-gather | bytes 417792 | tf_op jit(solution)/shard_map/all_gather | solution.py:10
  500.5 16.4 %fusion.2 = f32[64,144,4]{2,1,0:T(8,128)} fusion(f32[64,192]{1,0:T(8,128)S(1)} %copy.90, bf16[64,144,4,192]{3,2,1,0:T(4,128)(2,1)} %reshape.204), kind=kLoop, calls=%fused_computation.8 | loop fusion | flops 21196800 | bytes 14352384
  516.9 4.1 copy.87
  521.2 0.7 fusion.11
  522.5 2.5 convert_element_type.223
  525.0 3.3 multiply_reduce_fusion
  528.3 53.1 %all-reduce.9.cloned.1.call-done = bf16[9,8192]{1,0:T(8,128)(2,1)} async-done(((bf16[9,8192]{1,0:T(8,128)(2,1)}), bf16[9,8192]{1,0:T(8,128)(2,1)}) %all-reduce.9.cloned.1.call-update) | async-done | bytes 147472 | tf_op jit(solution)/shard_map/psum | solution.py:74
  581.4 1.7 multiply_reduce_fusion.6
  583.1 40.9 %psum.71 = f32[]{:T(128)} all-reduce(f32[]{:T(128)} %multiply_reduce_fusion.6), channel_id=1, replica_groups=mesh['cam'=16,'pts'=8] {'cam'}, use_global_device_ids=true, to_apply=%region_26.28 | all-reduce | flops 1 | bytes 8 | tf_op jit(solution)/shard_map/psum | solution.py:47
  625.4 2.1 multiply_subtract_fusion
  (75 shorter events, 9.9 us)
Async XLA Ops:
  7.2 163.4 %all-reduce.5.cloned.1.call-start = ((), (), s32[]{:S(2)}) async-start(), calls=%async_computation | async-start | bytes 524288 | tf_op jit(solution)/shard_map/psum | solution.py:74
  8.1 6.4 %copy-start.2 = (s32[64,1]{0,1:T(1,128)S(1)}, s32[64,1]{0,1:T(1,128)}, u32[]{:S(2)}) copy-start(s32[64,1]{0,1:T(1,128)} %param.15) | copy-start | bytes 772
  50.6 34.4 %copy-start.1 = (f32[3,3,4096]{2,1,0:T(4,128)S(1)}, f32[3,3,4096]{2,1,0:T(4,128)}, u32[]{:S(2)}) copy-start(f32[3,3,4096]{2,1,0:T(4,128)} %param.12) | copy-start | bytes 442372
  106.2 64.4 %copy-start = (f32[9,8192]{1,0:T(8,128)S(1)}, f32[9,8192]{1,0:T(8,128)}, u32[]{:S(2)}) copy-start(f32[9,8192]{1,0:T(8,128)} %param.9) | copy-start | bytes 884740
  110.1 264.4 %all-reduce.7.cloned.1.call-start = ((), (), s32[]{:S(2)}) async-start(), calls=%async_computation.1 | async-start | bytes 524288 | tf_op jit(solution)/shard_map/psum | solution.py:74
  318.1 263.3 %all-reduce.9.cloned.1.call-start = ((), (), s32[]{:S(2)}) async-start(), calls=%async_computation.2 | async-start | bytes 524288 | tf_op jit(solution)/shard_map/psum | solution.py:74
Sparse Core Ops, SparseCore 0:
  110.2 60.2 all-reduce.4
  318.2 56.2 all-reduce.6
  525.2 56.2 all-reduce.8
